TPU v7x, 256 devices: a whole 4x4x8 slice. The times are simulated.
256 devices in a mesh: ctx: 32 (over y, z), head: 8 (over x, core).
Axes of the slice: x: 4, y: 4, z: 8, core: 2. Of those that a mesh axis runs over, the one named last changes fastest.
Arguments:
- queries: bfloat16 [8192, 4096], P('ctx', 'head'), may hold values from -6 to 6
- key_rows: bfloat16 [8192, 4096], P('ctx', 'head'), may hold values from -0.5 to 0.5
- value_rows: bfloat16 [8192, 4096], P('ctx', 'head'), may hold values from -6 to 6
- doc_ids: int32 [8192], P('ctx'), may hold values from 0 to 15, never falling along the last dimension, each value on 1 to 2048 neighbouring positions
- out_grad: bfloat16 [8192, 6144], P(('ctx', 'head')), may hold values from -6 to 6
- out_weight: bfloat16 [4096, 6144], P('head', 'ctx'), may hold values from -0.09375 to 0.09375
Outputs:
- layer_out: bfloat16 [8192, 6144], P(('ctx', 'head'))
- query_grad: bfloat16 [8192, 4096], P('ctx', 'head')
- key_grad: bfloat16 [8192, 4096], P('ctx', 'head')
- value_grad: bfloat16 [8192, 4096], P('ctx', 'head')
- weight_grad: bfloat16 [4096, 6144], P(('head', 'ctx'))
Inputs may be any that keep to these rules, and one draw needn't show every extreme that they name: `doc_ids`: repository ids never fall along the sequence; each repository covers 1 to 2048 tokens, and one covers exactly that many.
All inputs are finite; a program needn't handle non-finite values.
Results may differ from a plain program's by a relative error of at most 0.025.
Values may be sent and summed in bfloat16 or wider, within the bound.
No kernel may reach another device: no remote copies, remote signals or barrier semaphores. Data moves between devices by JAX's collectives and lax.ppermute only.
A program may use at most 128 MiB of HBM per device.

v0:
```python
import jax
import jax.numpy as jnp
from jax import lax
from jax.sharding import PartitionSpec as P

HD = 128
EPSILON = 1e-05


def carried_in(x, axis, join, neutral, backward):
    count = lax.axis_size(axis)
    place = lax.axis_index(axis)
    ahead = count - 1 - place if backward else place
    gathered = jax.tree.map(
        lambda a, kind: lax.all_gather(a.astype(kind), axis),
        x,
        (jnp.bfloat16, jnp.bfloat16, jnp.bfloat16),
    )
    state = jax.tree.map(lambda a, e: jnp.zeros_like(a) + jnp.asarray(e, a.dtype), x, neutral)

    def one(lap, state):
        source = count - 1 - lap if backward else lap
        return join(
            state,
            jax.tree.map(
                lambda a, own: lax.dynamic_index_in_dim(a, source, 0, False).astype(own.dtype),
                gathered,
                x,
            ),
        )

    return lax.fori_loop(0, ahead, one, state)


def forward_link(earlier_part, later_part):
    early_first, early_last, early_state = earlier_part
    late_first, late_last, late_state = later_part
    late_empty = late_last < 0.0
    early_empty = early_last < 0.0
    linked = (early_last == late_first) & (late_first == late_last)
    joined = late_state + jnp.where(linked, early_state, jnp.float32(0.0))
    return (
        jnp.where(early_empty, late_first, early_first),
        jnp.where(late_empty, early_last, late_last),
        jnp.where(late_empty, early_state, joined),
    )


def backward_link(earlier_part, later_part):
    high_first, high_last, high_state = earlier_part
    low_first, low_last, low_state = later_part
    low_empty = low_last < 0.0
    high_empty = high_last < 0.0
    linked = (high_first == low_last) & (low_first == low_last)
    joined = low_state + jnp.where(linked, high_state, jnp.float32(0.0))
    return (
        jnp.where(low_empty, high_first, low_first),
        jnp.where(high_empty, low_last, high_last),
        jnp.where(low_empty, high_state, joined),
    )


def shards(queries, key_rows, value_rows, doc_ids, out_grad, out_weight):
    tok_count, full_width = queries.shape
    head_count = full_width // HD
    query_heads = queries.reshape(tok_count, head_count, HD)
    key_heads = key_rows.reshape(tok_count, head_count, HD)
    value_heads = value_rows.reshape(tok_count, head_count, HD)
    doc_values = doc_ids.astype(jnp.float32)
    first_doc = doc_values[:1]
    last_doc = doc_values[-1:]
    causal = jnp.tril(jnp.ones((tok_count, tok_count), dtype=bool))
    allowed = (causal & (doc_ids[:, None] == doc_ids[None, :]))[None]
    scores = jnp.einsum("thd,shd->hts", query_heads, key_heads, preferred_element_type=jnp.float32)
    weights = jnp.where(allowed, scores, jnp.float32(0.0)).astype(jnp.bfloat16)
    key_last = jnp.where(
        (doc_values == last_doc)[:, None, None], key_heads, jnp.zeros_like(key_heads)
    )
    local_state = jnp.einsum(
        "thd,the->hde", key_last, value_heads, preferred_element_type=jnp.float32
    )
    empty_marks = jnp.full((1,), -1.0, jnp.float32)
    identity = (empty_marks, empty_marks, jnp.zeros_like(local_state))
    prior_first, prior_last, prior_state = carried_in(
        (first_doc, last_doc, local_state), "ctx", forward_link, identity, False
    )
    row_mask = doc_values == prior_last
    prior_rounded = prior_state.astype(jnp.bfloat16)
    inter = jnp.einsum(
        "thd,hde->the", query_heads, prior_rounded, preferred_element_type=jnp.float32
    )
    mixed = jnp.einsum(
        "hts,she->the", weights, value_heads, preferred_element_type=jnp.float32
    ) + jnp.where(row_mask[:, None, None], inter, jnp.float32(0.0))
    inv_norm = lax.rsqrt(jnp.mean(mixed * mixed, axis=-1, keepdims=True) + EPSILON)
    normed = mixed * inv_norm
    normed_flat = normed.astype(jnp.bfloat16).reshape(tok_count, full_width)
    full_weight = lax.all_gather(out_weight, "ctx", axis=1, tiled=True)
    layer_out = lax.psum_scatter(
        jnp.dot(normed_flat, full_weight, preferred_element_type=jnp.float32).astype(jnp.bfloat16),
        "head",
        scatter_dimension=0,
        tiled=True,
    )
    grad_full = lax.all_gather(out_grad, "head", axis=0, tiled=True)
    grad_normed = lax.dot_general(
        grad_full, full_weight, (((1,), (1,)), ((), ())), preferred_element_type=jnp.float32
    ).reshape(tok_count, head_count, HD)
    mixed_grad = (
        inv_norm * (grad_normed - normed * jnp.mean(grad_normed * normed, axis=-1, keepdims=True))
    ).astype(jnp.bfloat16)
    weight_grad = lax.psum_scatter(
        lax.dot_general(
            normed_flat, grad_full, (((0,), (0,)), ((), ())), preferred_element_type=jnp.float32
        ).astype(jnp.bfloat16),
        "ctx",
        scatter_dimension=0,
        tiled=True,
    )
    query_first = jnp.where(
        (doc_values == first_doc)[:, None, None], query_heads, jnp.zeros_like(query_heads)
    )
    local_future = jnp.einsum(
        "thd,the->hde", query_first, mixed_grad, preferred_element_type=jnp.float32
    )
    later_first, later_last, future_state = carried_in(
        (first_doc, last_doc, local_future), "ctx", backward_link, identity, True
    )
    col_mask = (doc_values == later_first)[:, None, None]
    future_rounded = future_state.astype(jnp.bfloat16)
    grad_raw = jnp.einsum(
        "the,she->hts", mixed_grad, value_heads, preferred_element_type=jnp.float32
    )
    grad_scores = jnp.where(allowed, grad_raw, jnp.float32(0.0)).astype(jnp.bfloat16)
    query_grad = jnp.einsum(
        "hts,shd->thd", grad_scores, key_heads, preferred_element_type=jnp.float32
    ) + jnp.where(
        row_mask[:, None, None],
        jnp.einsum("the,hde->thd", mixed_grad, prior_rounded, preferred_element_type=jnp.float32),
        jnp.float32(0.0),
    )
    key_grad = jnp.einsum(
        "hts,thd->shd", grad_scores, query_heads, preferred_element_type=jnp.float32
    ) + jnp.where(
        col_mask,
        jnp.einsum("she,hde->shd", value_heads, future_rounded, preferred_element_type=jnp.float32),
        jnp.float32(0.0),
    )
    value_grad = jnp.einsum(
        "hts,the->she", weights, mixed_grad, preferred_element_type=jnp.float32
    ) + jnp.where(
        col_mask,
        jnp.einsum("shd,hde->she", key_heads, future_rounded, preferred_element_type=jnp.float32),
        jnp.float32(0.0),
    )
    return (
        layer_out,
        query_grad.astype(jnp.bfloat16).reshape(tok_count, full_width),
        key_grad.astype(jnp.bfloat16).reshape(tok_count, full_width),
        value_grad.astype(jnp.bfloat16).reshape(tok_count, full_width),
        weight_grad,
    )


def solution(mesh):
    return jax.shard_map(
        shards,
        mesh=mesh,
        in_specs=(
            P("ctx", "head"),
            P("ctx", "head"),
            P("ctx", "head"),
            P("ctx"),
            P(("ctx", "head"), None),
            P("head", "ctx"),
        ),
        out_specs=(
            P(("ctx", "head"), None),
            P("ctx", "head"),
            P("ctx", "head"),
            P("ctx", "head"),
            P(("head", "ctx"), None),
        ),
        check_vma=False,
    )
```

profile of v0, /device:TPU:2, one launch (start us, length us, event | category | flops | bytes accessed | tf_op | source)
XLA Modules:
  0.0 609.2 jit_solution(14436302235198908007)
XLA Ops:
  7.2 0.7 convert_element_type.105
  7.9 1.1 copy.86
  9.6 2.0 broadcast_compare_fusion.1
  11.6 0.9 convolution_convert_fusion.3
  12.5 0.7 all-gather.11.cloned.1.call-update
  13.3 0.7 all-gather.9.cloned.1.call-update
  14.0 1.3 dynamic-slice
  15.9 1.4 dynamic-update-slice
  17.3 1.4 dynamic-update-slice.1
  18.7 78.3 %all-reduce.2 = (bf16[32]{0:T(256)(128)(2,1)S(1)}, bf16[32]{0:T(256)(128)(2,1)S(1)}) all-reduce(bf16[32]{0:T(256)(128)(2,1)S(1)} %dynamic-update-slice, bf16[32]{0:T(256)(128)(2,1)S(1)} %dynamic-update-slice.1), channel_id=2, replica_groups=mesh['ctx'=32,'head'=8] {'ctx'}, use_global_device_ids=true, to_apply=%add | all-reduce | flops 64 | bytes 256
  97.0 1.1 copy.59
  98.1 0.9 fusion.22
  99.0 1.3 fusion.2
  101.0 24.8 %all-gather.11.cloned.1.call-done = bf16[256,6144]{1,0:T(8,128)(2,1)} async-done(((bf16[32,6144]{1,0:T(8,128)(2,1)}), bf16[256,6144]{1,0:T(8,128)(2,1)}) %all-gather.11.cloned.1.call-update) | async-done | bytes 3145744 | tf_op jit(solution)/shard_map/all_gather | solution.py:105
  125.8 92.5 %all-gather.9.cloned.1.call-done = bf16[512,6144]{0,1:T(8,128)(2,1)} async-done(((bf16[512,192]{0,1:T(8,128)(2,1)}), bf16[512,6144]{0,1:T(8,128)(2,1)}) %all-gather.9.cloned.1.call-update) | async-done | bytes 6291472 | tf_op jit(solution)/shard_map/all_gather | solution.py:98
  218.2 6.3 %multiply_reduce_fusion = (f32[256,4]{0,1:T(4,128)S(1)}, f32[256,512]{0,1:T(8,128)S(1)}) fusion(f32[256,4,128]{0,2,1:T(8,128)S(1)} %get-tuple-element.234, f32[256,4]{0,1:T(4,128)S(1)} %add_rsqrt_fusion, bf16[256,6144]{1,0:T(8,128)(2,1)} %all-gather.11.cloned.1.call-done, bf16[512,6144]{0,1:T(8,128)(2,1)} %all-gather.9.cloned.1.call-done), kind=kOutput, calls=%fused_computation.34 | convolution fusion | flops 1611004928 | bytes 10493952 | tf_op jit(solution)/shard_map/dot_general | solution.py:106
  224.7 0.9 convolution_convert_fusion.2
  225.6 6.4 %convolution_convert_fusion.1 = bf16[256,6144]{1,0:T(8,128)(2,1)} fusion(bf16[256,512]{0,1:T(8,128)(2,1)S(1)} %bitcast.132, bf16[512,6144]{0,1:T(8,128)(2,1)} %all-gather.9.cloned.1.call-done), kind=kOutput, calls=%fused_computation.9 | convolution fusion | flops 1612185600 | bytes 9699328 | tf_op jit(solution)/shard_map/dot_general | solution.py:100
  232.1 6.4 %convolution_convert_fusion = bf16[512,6144]{1,0:T(8,128)(2,1)} fusion(bf16[256,512]{0,1:T(8,128)(2,1)S(1)} %bitcast.133, bf16[256,6144]{1,0:T(8,128)(2,1)} %all-gather.11.cloned.1.call-done), kind=kOutput, calls=%fused_computation.8 | convolution fusion | flops 1613758464 | bytes 9699328 | tf_op jit(solution)/shard_map/dot_general | solution.py:113
  239.4 0.8 copy.50
  240.7 94.9 %all-gather.15.cloned.1.call-done = bf16[128,128,128]{2,1,0:T(8,128)(2,1)} async-done(((bf16[4,128,128]{2,1,0:T(8,128)(2,1)}), bf16[128,128,128]{2,1,0:T(8,128)(2,1)}) %all-gather.15.cloned.1.call-update) | async-done | bytes 4194320 | tf_op jit(solution)/shard_map/all_gather | solution.py:15
  335.7 158.6 %while.31 = (s32[]{:T(128)}, f32[1]{0:T(128)}, f32[4,128,128]{2,1,0:T(8,128)S(1)}, s32[]{:T(128)}, bf16[32,1]{0,1:T(2,128)(2,1)S(1)}, /*index=5*/bf16[32,1]{0,1:...) while((s32[]{:T(128)}, f32[1]{0:T(128)}, ...), condition=%wide.region_6.7_spmd, body=%wide.region_5.6_spmd.sunk | while | flops 262155 | bytes 655590 | solution.py:32
  335.7 0.7 constant_dynamic-slice_fusion.7
  339.7 1.0 fusion.69
  340.8 0.7 constant_dynamic-slice_fusion.7
  344.8 1.0 fusion.69
  345.9 0.7 constant_dynamic-slice_fusion.7
  350.0 1.0 fusion.69
  351.0 0.7 constant_dynamic-slice_fusion.7
  355.1 1.0 fusion.69
  360.2 1.0 fusion.69
  365.3 1.0 fusion.69
  366.4 0.7 constant_dynamic-slice_fusion.7
  370.4 1.0 fusion.69
  371.5 0.7 constant_dynamic-slice_fusion.7
  375.5 1.0 fusion.69
  376.6 0.7 constant_dynamic-slice_fusion.7
  380.7 1.0 fusion.69
  385.8 1.0 fusion.69
  386.8 0.7 constant_dynamic-slice_fusion.7
  390.9 1.0 fusion.69
  396.0 1.0 fusion.69
  401.1 1.0 fusion.69
  406.2 1.0 fusion.69
  411.3 1.0 fusion.69
  416.5 1.0 fusion.69
  421.6 1.0 fusion.69
  426.7 1.0 fusion.69
  431.8 1.0 fusion.69
  436.9 1.0 fusion.69
  442.0 1.1 fusion.69
  447.2 1.0 fusion.69
  452.3 1.0 fusion.69
  457.4 1.0 fusion.69
  462.5 1.0 fusion.69
  467.6 1.0 fusion.69
  472.7 1.0 fusion.69
  477.9 1.0 fusion.69
  483.0 1.0 fusion.69
  488.1 1.0 fusion.69
  493.2 1.0 fusion.69
  494.5 0.8 copy.51
  495.6 0.8 copy.52
  496.5 105.9 %reduce-scatter.5.cloned.1.call-done = bf16[16,6144]{1,0:T(8,128)(2,1)} async-done(((bf16[512,6144]{1,0:T(8,128)(2,1)}), bf16[16,6144]{1,0:T(8,128)(2,1)}) %reduce-scatter.5.cloned.1.call-update) | async-done | bytes 196624 | tf_op jit(solution)/shard_map/reduce_scatter | solution.py:112
  (62 shorter events, 19.5 us)
Async XLA Ops:
  7.2 4.4 copy-start
  7.2 93.4 %all-gather.13.cloned.1.call-start = ((), (), s32[]{:S(2)}) async-start(), calls=%async_computation.6 | async-start | bytes 4325376 | tf_op jit(solution)/shard_map/all_gather | solution.py:15
  11.6 89.1 %copy-start.2 = (s32[256]{0:T(256)S(1)}, s32[256]{0:T(256)}, u32[]{:S(2)}) copy-start(s32[256]{0:T(256)} %param.13) | copy-start | bytes 3076
  12.5 113.3 %all-gather.11.cloned.1.call-start = ((), (), s32[]{:S(2)}) async-start(), calls=%async_computation.4 | async-start | bytes 3538944 | tf_op jit(solution)/shard_map/all_gather | solution.py:105
  13.2 205.0 %all-gather.9.cloned.1.call-start = ((), (), s32[]{:S(2)}) async-start(), calls=%async_computation.2 | async-start | bytes 6488064 | tf_op jit(solution)/shard_map/all_gather | solution.py:98
  14.0 321.7 %all-gather.15.cloned.1.call-start = ((), (), s32[]{:S(2)}) async-start(), calls=%async_computation.7 | async-start | bytes 4325376 | tf_op jit(solution)/shard_map/all_gather | solution.py:15
  225.6 270.9 %reduce-scatter.3.cloned.1.call-start = ((), (), s32[]{:S(2)}) async-start(), calls=%async_computation.3 | async-start | bytes 3538944 | tf_op jit(solution)/shard_map/reduce_scatter | solution.py:99
  232.1 370.3 %reduce-scatter.5.cloned.1.call-start = ((), (), s32[]{:S(2)}) async-start(), calls=%async_computation.5 | async-start | bytes 6488064 | tf_op jit(solution)/shard_map/reduce_scatter | solution.py:112
  240.2 255.1 %copy-start.1 = (bf16[256,512]{1,0:T(8,128)(2,1)S(1)}, bf16[256,512]{1,0:T(8,128)(2,1)}, u32[]{:S(2)}) copy-start(bf16[256,512]{1,0:T(8,128)(2,1)} %param.11) | copy-start | bytes 786436
Sparse Core Ops, SparseCore 0:
  12.6 84.7 all-gather.12
  99.3 26.4 all-gather.10
  128.3 89.8 all-gather.8
  225.7 109.8 all-gather.14
  338.6 32.1 reduce-scatter.2
  375.2 227.1 reduce-scatter.4
where the time goes:
time: 612 us; the launch traced here: 609 us
  waiting for transfers between devices  320 us (52%)
  loops' own time  105 us (17%)
  blocking collectives  78.3 us (13%)
  other arithmetic  36.1 us (6%)
  local copies, waits for them, and re-layouts  30.8 us (5%)
  matrix products  24.5 us (4%)
  between operations  14.3 us (2%)
    reduce_scatter x1, waiting for transfers between devices, shards(): lax.psum_scatter(lax.dot_general(normed_flat, grad_full, (((0,), (0,)), (...  106 us
    another operation x2, loops' own time, carried_in(): return lax.fori_loop(0, ahead, one, state)  105 us
    all_gather x2, waiting for transfers between devices, carried_in(): lax.all_gather(a.astype(kind), axis)  95 us
    all_gather x1, waiting for transfers between devices, shards(): full_weight = lax.all_gather(out_weight, 'ctx', axis=1, tiled=True)  92.5 us
    unnamed x1, blocking collectives  78.3 us
    select_n x31, other arithmetic, backward_link(): jnp.where(low_empty, high_state, joined)  32.4 us
    all_gather x1, waiting for transfers between devices, shards(): grad_full = lax.all_gather(out_grad, 'head', axis=0, tiled=True)  24.8 us
    dynamic_slice x31, local copies, waits for them, and re-layouts, one(): lax.dynamic_index_in_dim(a, source, 0, False).astype(own.dtype)  20.8 us
  transfers between devices with their start and end apart: 6, of which 4 were waited for; matrix products, arithmetic and copies ran while one was open for 13% of the time, Pallas kernels for 0%

commit v1 on v0

--- a/solution.py
+++ b/solution.py
@@ -95,7 +95,12 @@
     inv_norm = lax.rsqrt(jnp.mean(mixed * mixed, axis=-1, keepdims=True) + EPSILON)
     normed = mixed * inv_norm
     normed_flat = normed.astype(jnp.bfloat16).reshape(tok_count, full_width)
-    full_weight = lax.all_gather(out_weight, "ctx", axis=1, tiled=True)
+    full_weight = jnp.concatenate(
+        lax.all_to_all(
+            jnp.stack([out_weight for _ in range(lax.axis_size("ctx"))], 0), "ctx", 0, 0
+        ),
+        1,
+    )
     layer_out = lax.psum_scatter(
         jnp.dot(normed_flat, full_weight, preferred_element_type=jnp.float32).astype(jnp.bfloat16),
         "head",

time: 612 us -> 779 us (1.27)
  blocking collectives: 78.3 us -> 224 us
  starting transfers between devices: 0.24 us -> 11.9 us
  local copies, waits for them, and re-layouts: 30.8 us -> 41.4 us
    unnamed x1, blocking collectives: 78.3 us -> 224 us
    all_gather x2, waiting for transfers between devices: 95 us -> 212 us  [carried_in(): lax.all_gather(a.astype(kind), axis)]
    all_gather x1 -> x0, waiting for transfers between devices: 92.5 us -> none  [shards(): full_weight = lax.all_gather(out_weight, 'ctx', axis=1, tiled=True)]
    all_gather x1, waiting for transfers between devices: 24.8 us -> 0.01 us  [shards(): grad_full = lax.all_gather(out_grad, 'head', axis=0, tiled=True)]
    all_to_all x0 -> x1, starting transfers between devices: none -> 11.7 us  [shards(): lax.all_to_all(jnp.stack([out_weight for _ in range(lax.axis_size('ctx'))...]
    dot_general x0 -> x1, local copies, waits for them, and re-layouts: none -> 9.75 us  [shards(): lax.dot_general(grad_full, full_weight, (((1,), (1,)), ((), ())), preferr...]
  transfers between devices with their start and end apart: 6 -> 6, of which waited for: 4 -> 2; matrix products, arithmetic and copies ran while one was open for 13% -> 11% of each run, Pallas kernels for 0% -> 0%
where the time goes in v1:
time: 779 us; the launch traced here: 777 us
  waiting for transfers between devices  326 us (42%)
  blocking collectives  224 us (29%)
  loops' own time  101 us (13%)
  local copies, waits for them, and re-layouts  41.4 us (5%)
  other arithmetic  35.3 us (5%)
  matrix products  23.6 us (3%)
  between operations  14 us (2%)
  starting transfers between devices  11.9 us (2%)
    unnamed x1, blocking collectives  224 us
    all_gather x2, waiting for transfers between devices, carried_in(): lax.all_gather(a.astype(kind), axis)  212 us
    reduce_scatter x1, waiting for transfers between devices, shards(): lax.psum_scatter(lax.dot_general(normed_flat, grad_full, (((0,), (0,)), (...  112 us
    another operation x2, loops' own time, carried_in(): return lax.fori_loop(0, ahead, one, state)  101 us
    select_n x31, other arithmetic, backward_link(): jnp.where(low_empty, high_state, joined)  32.4 us
    dynamic_slice x31, local copies, waits for them, and re-layouts, one(): lax.dynamic_index_in_dim(a, source, 0, False).astype(own.dtype)  19 us
  transfers between devices with their start and end apart: 6, of which 2 were waited for; matrix products, arithmetic and copies ran while one was open for 11% of the time, Pallas kernels for 0%

profile of v1, /device:TPU:2, one launch (start us, length us, event | category | flops | bytes accessed | tf_op | source)
XLA Modules:
  0.0 776.9 jit_solution(12155005538287813001)
XLA Ops:
  7.2 0.7 convert_element_type.105
  8.5 1.1 copy.108
  9.6 2.0 broadcast_compare_fusion.1
  11.6 0.9 convolution_convert_fusion.3
  12.5 4.3 stack.2
  16.8 11.7 %all-to-all-start = ((bf16[32,512,192]{1,2,0:T(8,128)(2,1)}), bf16[32,512,192]{1,2,0:T(8,128)(2,1)}, u32[]{:S(2)}, u32[]{:S(2)}) async-start(bf16[32,512,192]{1,2,0:T(8,128)(2,1)} %stack.2), calls=%async_computation | async-start | bytes 12582912 | tf_op jit(solution)/shard_map/all_to_all | solution.py:99
  28.6 0.7 all-gather.8.cloned.1.call-update
  30.5 1.4 dynamic-update-slice
  31.9 1.4 dynamic-update-slice.1
  33.3 224.4 %all-reduce.2 = (bf16[32]{0:T(256)(128)(2,1)S(1)}, bf16[32]{0:T(256)(128)(2,1)S(1)}) all-reduce(bf16[32]{0:T(256)(128)(2,1)S(1)} %dynamic-update-slice, bf16[32]{0:T(256)(128)(2,1)S(1)} %dynamic-update-slice.1), channel_id=2, replica_groups=mesh['ctx'=32,'head'=8] {'ctx'}, use_global_device_ids=true, to_apply=%add | all-reduce | flops 64 | bytes 256
  259.1 9.8 %dot_general.52 = bf16[4,128,6144]{1,0,2:T(4,128)(2,1)} reshape(bf16[512,32,192]{0,2,1:T(8,128)(2,1)} %bitcast.23) | data formatting | bytes 12582912 | tf_op jit(solution)/shard_map/dot_general | solution.py:111
  268.8 6.3 multiply_reduce_fusion
  275.2 0.9 convolution_convert_fusion.2
  276.2 6.4 convolution_convert_fusion.1
  282.7 6.4 convolution_convert_fusion
  290.0 0.8 copy.71
  291.3 212.5 %all-gather.12.cloned.1.call-done = bf16[128,128,128]{2,1,0:T(8,128)(2,1)} async-done(((bf16[4,128,128]{2,1,0:T(8,128)(2,1)}), bf16[128,128,128]{2,1,0:T(8,128)(2,1)}) %all-gather.12.cloned.1.call-update) | async-done | bytes 4194320 | tf_op jit(solution)/shard_map/all_gather | solution.py:15
  503.8 152.1 %while.31 = (s32[]{:T(128)}, f32[1]{0:T(128)}, f32[4,128,128]{2,1,0:T(8,128)S(1)}, s32[]{:T(128)}, bf16[32,1]{0,1:T(2,128)(2,1)S(1)}, /*index=5*/bf16[32,1]{0,1:...) while((s32[]{:T(128)}, f32[1]{0:T(128)}, ...), condition=%wide.region_6.7_spmd, body=%wide.region_5.6_spmd.sunk | while | flops 262155 | bytes 655574 | solution.py:32
  503.8 0.6 constant_dynamic-slice_fusion.7
  507.0 1.0 fusion.70
  508.7 0.6 constant_dynamic-slice_fusion.7
  511.9 1.0 fusion.70
  513.6 0.6 constant_dynamic-slice_fusion.7
  516.8 1.0 fusion.70
  518.5 0.6 constant_dynamic-slice_fusion.7
  521.7 1.0 fusion.70
  523.4 0.6 constant_dynamic-slice_fusion.7
  526.6 1.0 fusion.70
  528.3 0.6 constant_dynamic-slice_fusion.7
  531.5 1.0 fusion.70
  536.4 1.0 fusion.70
  538.2 0.6 constant_dynamic-slice_fusion.7
  541.3 1.0 fusion.70
  546.2 1.0 fusion.70
  551.1 1.0 fusion.70
  556.0 1.0 fusion.70
  560.9 1.0 fusion.70
  562.7 0.6 constant_dynamic-slice_fusion.7
  565.8 1.0 fusion.70
  570.8 1.0 fusion.70
  575.7 1.0 fusion.70
  580.6 1.0 fusion.70
  582.3 0.6 constant_dynamic-slice_fusion.7
  585.5 1.0 fusion.70
  590.4 1.0 fusion.70
  595.3 1.0 fusion.70
  600.2 1.0 fusion.70
  605.1 1.0 fusion.70
  610.0 1.0 fusion.70
  611.7 0.6 constant_dynamic-slice_fusion.7
  614.9 1.0 fusion.70
  619.8 1.0 fusion.70
  621.5 0.6 constant_dynamic-slice_fusion.7
  624.7 1.0 fusion.70
  629.6 1.0 fusion.70
  634.5 1.0 fusion.70
  639.4 1.0 fusion.70
  644.3 1.0 fusion.70
  646.1 0.6 constant_dynamic-slice_fusion.7
  649.3 1.0 fusion.70
  654.2 1.0 fusion.70
  656.2 0.8 copy.73
  657.2 0.8 copy.72
  658.1 112.3 %reduce-scatter.5.cloned.1.call-done = bf16[16,6144]{1,0:T(8,128)(2,1)} async-done(((bf16[512,6144]{1,0:T(8,128)(2,1)}), bf16[16,6144]{1,0:T(8,128)(2,1)}) %reduce-scatter.5.cloned.1.call-update) | async-done | bytes 196624 | tf_op jit(solution)/shard_map/reduce_scatter | solution.py:117
  (67 shorter events, 16.9 us)
Async XLA Ops:
  7.2 4.4 copy-start
  7.2 251.5 %all-gather.10.cloned.1.call-start = ((), (), s32[]{:S(2)}) async-start(), calls=%async_computation.6 | async-start | bytes 4325376 | tf_op jit(solution)/shard_map/all_gather | solution.py:15
  16.7 12.6 %copy-start.4 = (u32[256]{0:T(256)S(1)}, u32[256]{0:T(256)}, u32[]{:S(2)}) copy-start(u32[256]{0:T(256)} %constant.98) | copy-start | bytes 3076
  16.8 241.0 %copy-start.2 = (bf16[256,512]{1,0:T(8,128)(2,1)S(1)}, bf16[256,512]{1,0:T(8,128)(2,1)}, u32[]{:S(2)}) copy-start(bf16[256,512]{1,0:T(8,128)(2,1)} %param.10) | copy-start | bytes 786436
  16.8 241.1 %copy-start.3 = (s32[256]{0:T(256)S(1)}, s32[256]{0:T(256)}, u32[]{:S(2)}) copy-start(s32[256]{0:T(256)} %param.13) | copy-start | bytes 3076
  16.8 241.2 %copy-start.1 = (bf16[256,512]{1,0:T(8,128)(2,1)S(1)}, bf16[256,512]{1,0:T(8,128)(2,1)}, u32[]{:S(2)}) copy-start(bf16[256,512]{1,0:T(8,128)(2,1)} %param.11) | copy-start | bytes 786436
  16.8 242.3 %all-to-all-start = ((bf16[32,512,192]{1,2,0:T(8,128)(2,1)}), bf16[32,512,192]{1,2,0:T(8,128)(2,1)}, u32[]{:S(2)}, u32[]{:S(2)}) async-start(bf16[32,512,192]{1,2,0:T(8,128)(2,1)} %stack.2), calls=%async_computation | async-start | bytes 12582912 | tf_op jit(solution)/shard_map/all_to_all | solution.py:99
  28.5 240.3 %all-gather.8.cloned.1.call-start = ((), (), s32[]{:S(2)}) async-start(), calls=%async_computation.4 | async-start | bytes 3538944 | tf_op jit(solution)/shard_map/all_gather | solution.py:110
  29.3 474.5 %all-gather.12.cloned.1.call-start = ((), (), s32[]{:S(2)}) async-start(), calls=%async_computation.7 | async-start | bytes 4325376 | tf_op jit(solution)/shard_map/all_gather | solution.py:15
  276.2 381.9 %reduce-scatter.3.cloned.1.call-start = ((), (), s32[]{:S(2)}) async-start(), calls=%async_computation.3 | async-start | bytes 3538944 | tf_op jit(solution)/shard_map/reduce_scatter | solution.py:104
  282.7 487.7 %reduce-scatter.5.cloned.1.call-start = ((), (), s32[]{:S(2)}) async-start(), calls=%async_computation.5 | async-start | bytes 6488064 | tf_op jit(solution)/shard_map/reduce_scatter | solution.py:117
Sparse Core Ops, SparseCore 0:
  12.6 136.4 all-gather.9
  150.9 37.8 all-gather.7
  276.3 227.4 all-gather.11
  506.7 32.1 reduce-scatter.2
  543.4 226.9 reduce-scatter.4
